TPU v7x, 32 devices: a whole 2x2x4 slice. The times are simulated.
32 devices in a mesh: group: 2 (over y), tile: 4 (over x, core), seq: 4 (over z).
Axes of the slice: x: 2, y: 2, z: 4, core: 2. Of those that a mesh axis runs over, the one named last changes fastest.
Arguments:
- hidden: bfloat16 [8, 1024, 3072], P(('group', 'tile'), 'seq'), parts along dimension 0
- modulation: float32 [10, 3072], P('group'), parts along dimension 0, may hold values from -3 to 3
- w_qkv: bfloat16 [3072, 9216], P('tile', 'seq')
- w_out: bfloat16 [3072, 3072], P('seq', 'tile'), may hold values from -0.109375 to 0.109375
- w_head: bfloat16 [3072, 64], replicated, may hold values from -0.109375 to 0.109375
- latent: float32 [8, 1024, 64], P(('group', 'tile'), 'seq'), parts along dimension 0, may hold values from -6 to 6
- weights_int: int32 [8, 1024], P(('group', 'tile'), 'seq'), parts along dimension 0, may hold values from 1 to 8
- step_index: int32 [2], P('group'), parts along dimension 0, may hold values from 0 to 13
Outputs:
- stepped: float32 [8, 1024, 64], P(('group', 'tile'), 'seq'), parts along dimension 0
- clean: float32 [8, 1024, 64], P(('group', 'tile'), 'seq'), parts along dimension 0
There are 2 independent parts, one for each index of `group`. A program takes and returns all parts, laid end to end along the dimension named above; an argument that names none is the same for every part. Nothing has to cross between parts.
All inputs are finite; a program needn't handle non-finite values.
Results may differ from a plain program's by a relative error of at most 0.0055.
Values may be sent and summed in bfloat16 or wider, within the bound.
A program may use at most 64 MiB of HBM per device.

v0:
```python
import math
import jax
import jax.numpy as jnp
from jax import lax
from jax.sharding import PartitionSpec as P

HD = 128
NSTEPS = 28


def shifted(value, axis, steps):
    count = lax.axis_size(axis)
    leading, last = (max(0, -steps), min(count, count - steps))
    return lax.ppermute(value, axis, [(source, source + steps) for source in range(leading, last)])


def layer_norm(values):
    mean = jnp.mean(values, axis=-1, keepdims=True)
    centred = values - mean
    spread = jnp.mean(centred * centred, axis=-1, keepdims=True)
    return centred * lax.rsqrt(spread + 1e-06)


def root_norm(values):
    return values * lax.rsqrt(jnp.mean(values * values, axis=-1, keepdims=True) + 1e-06)


def noise_level(index, steps):
    level = 1.0 - index / steps
    return 3.0 * level / (1.0 + 2.0 * level)


def shards(hidden, modulation, w_qkv, w_out, w_head, latent, weights_int, step_index):
    local = hidden[0].astype(jnp.float32)
    norm_in = (layer_norm(local) * (1.0 + modulation[1]) + modulation[0]).astype(jnp.bfloat16)
    gathered = lax.all_gather(norm_in, "seq", axis=0, tiled=True)
    length = gathered.shape[0]
    heads_here = w_qkv.shape[1] // (3 * HD)
    projected = jnp.dot(
        gathered,
        lax.all_gather(w_qkv, "tile", axis=0, tiled=True),
        preferred_element_type=jnp.float32,
    )
    full_out = lax.all_gather(w_out, "tile", axis=1, tiled=True)
    projected = projected.reshape(length, heads_here, 3, HD)
    queries = root_norm(projected[:, :, 0]).astype(jnp.bfloat16)
    keys = root_norm(projected[:, :, 1]).astype(jnp.bfloat16)
    values = projected[:, :, 2].astype(jnp.bfloat16)
    block = min(512, length)
    scale = 1.0 / math.sqrt(HD)
    pieces = []
    for first in range(0, length, block):
        scores = (
            jnp.einsum(
                "qhe,khe->hqk",
                queries[first : first + block],
                keys,
                preferred_element_type=jnp.float32,
            )
            * scale
        )
        expo = jnp.exp(scores)
        probs = (expo / jnp.sum(expo, axis=-1, keepdims=True)).astype(jnp.bfloat16)
        pieces.append(
            jnp.einsum("hqk,khe->qhe", probs, values, preferred_element_type=jnp.float32).astype(
                jnp.bfloat16
            )
        )
    attended = jnp.concatenate(pieces, axis=0).reshape(length, heads_here * HD)
    summed = lax.psum_scatter(
        jnp.dot(attended, full_out, preferred_element_type=jnp.float32).astype(jnp.bfloat16),
        "seq",
        scatter_dimension=0,
        tiled=True,
    ).astype(jnp.float32)
    mixed = local + modulation[2] * summed
    norm_out = (layer_norm(mixed) * (1.0 + modulation[4]) + modulation[3]).astype(jnp.bfloat16)
    velocity = jnp.dot(norm_out, w_head, preferred_element_type=jnp.float32)
    index = step_index[0].astype(jnp.float32)
    now = noise_level(index, NSTEPS)
    after = noise_level(index + 1.0, NSTEPS)
    base = latent[0]
    weight = weights_int[0].astype(jnp.float32)
    moved = base + (after - now) * velocity
    guess = base - now * velocity
    weighted = jnp.concatenate([moved, guess], axis=1) * weight[:, None]
    seq_count = lax.axis_size("seq")
    place = lax.axis_index("seq")
    prev_tile = (
        shifted(weighted.astype(jnp.bfloat16), "tile", 1).astype(weighted.dtype),
        shifted(weight.astype(jnp.bfloat16), "tile", 1).astype(weight.dtype),
    )
    prev_sums, prev_weight = (
        shifted(prev_tile[0].astype(jnp.bfloat16), "seq", -(seq_count - 2)).astype(jnp.float32),
        shifted(prev_tile[1].astype(jnp.bfloat16), "seq", -(seq_count - 2)).astype(jnp.float32),
    )
    next_tile = (
        shifted(weighted.astype(jnp.bfloat16), "tile", -1).astype(weighted.dtype),
        shifted(weight.astype(jnp.bfloat16), "tile", -1).astype(weight.dtype),
    )
    next_sums, next_weight = (
        shifted(next_tile[0].astype(jnp.bfloat16), "seq", seq_count - 2).astype(jnp.float32),
        shifted(next_tile[1].astype(jnp.bfloat16), "seq", seq_count - 2).astype(jnp.float32),
    )
    take_prev = place < 2
    take_next = place >= seq_count - 2
    totals = weighted + jnp.where(take_prev, prev_sums, 0.0) + jnp.where(take_next, next_sums, 0.0)
    norms = weight + jnp.where(take_prev, prev_weight, 0.0) + jnp.where(take_next, next_weight, 0.0)
    joined = totals / norms[:, None]
    channels = velocity.shape[1]
    return (joined[None, :, :channels], joined[None, :, channels:])


def solution(mesh):
    in_specs = (
        P(("group", "tile"), "seq", None),
        P("group", None),
        P("tile", "seq"),
        P("seq", "tile"),
        P(),
        P(("group", "tile"), "seq", None),
        P(("group", "tile"), "seq"),
        P("group"),
    )
    out_specs = (P(("group", "tile"), "seq", None), P(("group", "tile"), "seq", None))
    return jax.shard_map(shards, mesh=mesh, in_specs=in_specs, out_specs=out_specs, check_vma=False)
```

profile of v0, /device:TPU:26, one launch (start us, length us, event | category | flops | bytes accessed | tf_op | source)
XLA Modules:
  0.0 437.2 jit_solution(16859526870282650366)
XLA Ops:
  7.2 1.9 fusion.30
  9.1 1.7 convert_reduce_fusion
  10.8 2.0 fusion.8
  12.8 1.9 fusion.11
  14.8 0.7 all-gather.6.cloned.1.call-update
  16.3 112.1 %all-gather.4.cloned.1.call-done = bf16[1024,3072]{1,0:T(8,128)(2,1)} async-done(((bf16[256,3072]{1,0:T(8,128)(2,1)}), bf16[1024,3072]{1,0:T(8,128)(2,1)}) %all-gather.4.cloned.1.call-update) | async-done | bytes 6291472 | tf_op jit(solution)/shard_map/all_gather | solution.py:36
  128.4 92.7 %all-gather.6.cloned.1.call-done = bf16[3072,2304]{1,0:T(8,128)(2,1)} async-done(((bf16[768,2304]{1,0:T(8,128)(2,1)}), bf16[3072,2304]{1,0:T(8,128)(2,1)}) %all-gather.6.cloned.1.call-update) | async-done | bytes 14155792 | tf_op jit(solution)/shard_map/all_gather | solution.py:41
  221.1 19.6 %fusion.31 = f32[1024,2304]{0,1:T(8,128)S(1)} fusion(bf16[1024,3072]{1,0:T(8,128)(2,1)} %all-gather.4.cloned.1.call-done, bf16[3072,2304]{1,0:T(8,128)(2,1)} %all-gather.6.cloned.1.call-done), kind=kOutput, calls=%fused_computation.60 | convolution fusion | flops 14495514624 | bytes 29884416 | tf_op jit(solution)/shard_map/dot_general | solution.py:39
  240.7 3.5 copy-done.3
  244.2 2.0 slice.50
  246.3 3.6 copy.21
  249.9 2.9 fusion.12
  252.8 2.3 multiply_reduce_fusion.1
  255.2 1.0 fusion.13
  256.2 8.2 %fusion = (f32[6,512]{1,0:T(8,128)S(1)}, f32[6,512,1024]{2,1,0:T(8,128)}) fusion(f32[1024,6,3,128]{0,3,2,1:T(8,128)} %bitcast.78, f32[1024,6]{0,1:T(8,128)S(1)} %add_rsqrt_fusion, bf16[1024,6,128]{2,0,1:T(8,128)(2,1)S(1)} %fusion.13), kind=kOutput, calls=%fused_computation.4 | convolution fusion | flops 813167616 | bytes 16560128 | tf_op jit(solution)/shard_map/qhe,khe->hqk/dot_general | solution.py:54
  264.5 2.7 fusion.1
  267.1 6.0 %fusion.19 = bf16[512,6,128]{0,2,1:T(8,128)(2,1)S(1)} fusion(f32[6,512,1024]{2,1,0:T(8,128)} %get-tuple-element.14, f32[6,512]{1,0:T(8,128)S(1)} %get-tuple-element.13, f32[1024,6,3,128]{0,3,2,1:T(8,128)S(1)} %bitcast.82), kind=kOutput, calls=%fused_computation.35 | convolution fusion | flops 815136768 | bytes 14958592 | tf_op jit(solution)/shard_map/hqk,khe->qhe/dot_general | solution.py:65
  273.1 2.9 fusion.20
  276.3 9.5 %convolution_convert_fusion = bf16[1024,3072]{1,0:T(8,128)(2,1)} fusion(bf16[1024,768]{0,1:T(8,128)(2,1)S(1)} %bitcast.84, bf16[768,3072]{1,0:T(8,128)(2,1)} %all-gather.8.cloned.1.call-done), kind=kOutput, calls=%fused_computation.8 | convolution fusion | flops 4834983936 | bytes 12582912 | tf_op jit(solution)/shard_map/dot_general | solution.py:71
  286.6 110.6 %reduce-scatter.2.cloned.1.call-done = bf16[256,3072]{1,0:T(8,128)(2,1)} async-done(((bf16[1024,3072]{1,0:T(8,128)(2,1)}), bf16[256,3072]{1,0:T(8,128)(2,1)}) %reduce-scatter.2.cloned.1.call-update) | async-done | bytes 1572880 | tf_op jit(solution)/shard_map/reduce_scatter | solution.py:70
  397.2 2.1 fusion.14
  399.4 0.8 multiply_reduce_fusion
  400.2 1.1 bitcast_add_fusion
  401.3 1.9 collective-permute-start
  403.3 3.6 collective-permute-start.2
  406.9 1.9 collective-permute-start.4
  408.9 3.6 collective-permute-start.6
  412.5 2.9 collective-permute-start.5
  415.5 1.3 collective-permute-start.7
  416.8 5.4 %collective-permute-start.1 = (bf16[256,128]{0,1:T(8,128)(2,1)S(1)}, bf16[256,128]{0,1:T(8,128)(2,1)S(1)}, u32[]{:S(2)}, u32[]{:S(2)}) collective-permute-start(bf16[256,128]{0,1:T(8,128)(2,1)S(1)} %collective-permute-done), channel_id=1, source_target_pairs={{2,0},{3,1},{6,4},{7,5},{10,8},{11,9},{14,12},{15,13},{18,16},{19,... | collective-permute-start | bytes 196616 | tf_op jit(solution)/shard_map/ppermute | solution.py:14
  422.2 1.3 collective-permute-start.3
  424.1 5.9 %collective-permute-done.3 = bf16[256,128]{0,1:T(8,128)(2,1)S(1)} collective-permute-done((bf16[256,128]{0,1:T(8,128)(2,1)S(1)}, bf16[256,128]{0,1:T(8,128)(2,1)S(1)}, u32[]{:S(2)}, u32[]{:S(2)}) %collective-permute-start.3) | collective-permute-done | bytes 65568 | tf_op jit(solution)/shard_map/ppermute | solution.py:14
  (52 shorter events, 2.5 us)
Async XLA Ops:
  7.2 393.0 %copy-start = (bf16[3072,64]{0,1:T(8,128)(2,1)S(1)}, bf16[3072,64]{0,1:T(8,128)(2,1)}, u32[]{:S(2)}) copy-start(bf16[3072,64]{0,1:T(8,128)(2,1)} %param.12) | copy-start | bytes 1179652
  7.2 5.6 %copy-start.1 = (bf16[1,256,3072]{2,1,0:T(8,128)(2,1)S(1)}, bf16[1,256,3072]{2,1,0:T(8,128)(2,1)}, u32[]{:S(2)}) copy-start(bf16[1,256,3072]{2,1,0:T(8,128)(2,1)} %param.8) | copy-start | bytes 4718596
  7.2 121.2 %all-gather.4.cloned.1.call-start = ((), (), s32[]{:S(2)}) async-start(), calls=%async_computation.1 | async-start | bytes 7864320 | tf_op jit(solution)/shard_map/all_gather | solution.py:36
  14.8 206.3 %all-gather.6.cloned.1.call-start = ((), (), s32[]{:S(2)}) async-start(), calls=%async_computation.2 | async-start | bytes 17694720 | tf_op jit(solution)/shard_map/all_gather | solution.py:41
  15.5 260.8 %all-gather.8.cloned.1.call-start = ((), (), s32[]{:S(2)}) async-start(), calls=%async_computation.3 | async-start | bytes 5898240 | tf_op jit(solution)/shard_map/all_gather | solution.py:44
  16.3 381.0 %reduce-scatter.2.cloned.1.call-start = ((), (), s32[]{:S(2)}) async-start(), calls=%async_computation.4 | async-start | bytes 7864320 | tf_op jit(solution)/shard_map/reduce_scatter | solution.py:70
  240.7 3.6 copy-start.3
  249.9 5.3 %copy-start.2 = (f32[1024,6,1,128]{3,0,1,2:T(8,128)S(1)}, f32[1024,6,1,128]{3,0,1,2:T(8,128)}, u32[]{:S(2)}) copy-start(f32[1024,6,1,128]{3,0,1,2:T(8,128)} %copy.21) | copy-start | bytes 9437188
  255.2 9.2 %slice-start = ((s8[9437184]{0:T(1024)(128)(4,1)}), s8[4194304]{0:T(1024)(128)(4,1)S(1)}, s32[]{:S(2)}) async-start(s8[9437184]{0:T(1024)(128)(4,1)} %bitcast.79), calls=%async_computation.5 | async-start | bytes 8388608
  256.2 8.3 %slice-start.1 = ((s8[9437184]{0:T(1024)(128)(4,1)}), s8[4194304]{0:T(1024)(128)(4,1)S(1)}, s32[]{:S(2)}) async-start(s8[9437184]{0:T(1024)(128)(4,1)} %bitcast.79), calls=%async_computation.6 | async-start | bytes 8388608
  256.2 8.2 %slice-start.2 = ((s8[9437184]{0:T(1024)(128)(4,1)}), s8[1048576]{0:T(1024)(128)(4,1)S(1)}, s32[]{:S(2)}) async-start(s8[9437184]{0:T(1024)(128)(4,1)} %bitcast.79), calls=%async_computation.7 | async-start | bytes 2097152
  285.8 0.7 copy-start.7
  397.2 2.1 copy-start.4
  397.2 3.0 copy-start.5
  397.2 3.0 copy-start.6
  397.2 3.0 copy-start.8
  401.3 15.4 %collective-permute-start = (bf16[256,128]{0,1:T(8,128)(2,1)S(1)}, bf16[256,128]{0,1:T(8,128)(2,1)S(1)}, u32[]{:S(2)}, u32[]{:S(2)}) collective-permute-start(bf16[256,128]{0,1:T(8,128)(2,1)S(1)} %fusion.27), channel_id=1, source_target_pairs={{0,4},{4,8},{8,12},{1,5},{5,9},{9,13},{2,6},{6,10},{10,14},{3,7},{... | collective-permute-start | bytes 196616 | tf_op jit(solution)/shard_map/ppermute | solution.py:14
  403.3 19.0 %collective-permute-start.2 = (bf16[256,128]{0,1:T(8,128)(2,1)S(1)}, bf16[256,128]{0,1:T(8,128)(2,1)S(1)}, u32[]{:S(2)}, u32[]{:S(2)}) collective-permute-start(bf16[256,128]{0,1:T(8,128)(2,1)S(1)} %fusion.27), channel_id=1, source_target_pairs={{4,0},{8,4},{12,8},{5,1},{9,5},{13,9},{6,2},{10,6},{14,10},{7,3},{... | collective-permute-start | bytes 196616 | tf_op jit(solution)/shard_map/ppermute | solution.py:14
  406.9 5.6 %collective-permute-start.4 = (bf16[256]{0:T(256)(128)(2,1)S(1)}, bf16[256]{0:T(256)(128)(2,1)S(1)}, u32[]{:S(2)}, u32[]{:S(2)}) collective-permute-start(bf16[256]{0:T(256)(128)(2,1)S(1)} %convert_element_type.109), channel_id=1, source_target_pairs={{0,4},{4,8},{8,12},{1,5},{5,9},{9,13},{2,6},{6,10},{10,14},{3,7},{... | collective-permute-start | bytes 1544 | tf_op jit(solution)/shard_map/ppermute | solution.py:14
  408.9 6.6 %collective-permute-start.6 = (bf16[256]{0:T(256)(128)(2,1)S(1)}, bf16[256]{0:T(256)(128)(2,1)S(1)}, u32[]{:S(2)}, u32[]{:S(2)}) collective-permute-start(bf16[256]{0:T(256)(128)(2,1)S(1)} %convert_element_type.109), channel_id=1, source_target_pairs={{4,0},{8,4},{12,8},{5,1},{9,5},{13,9},{6,2},{10,6},{14,10},{7,3},{... | collective-permute-start | bytes 1544 | tf_op jit(solution)/shard_map/ppermute | solution.py:14
  412.5 11.0 %collective-permute-start.5 = (bf16[256]{0:T(256)(128)(2,1)S(1)}, bf16[256]{0:T(256)(128)(2,1)S(1)}, u32[]{:S(2)}, u32[]{:S(2)}) collective-permute-start(bf16[256]{0:T(256)(128)(2,1)S(1)} %collective-permute-done.4), channel_id=1, source_target_pairs={{2,0},{3,1},{6,4},{7,5},{10,8},{11,9},{14,12},{15,13},{18,16},{19,... | collective-permute-start | bytes 1544 | tf_op jit(solution)/shard_map/ppermute | solution.py:14
  415.5 8.1 %collective-permute-start.7 = (bf16[256]{0:T(256)(128)(2,1)S(1)}, bf16[256]{0:T(256)(128)(2,1)S(1)}, u32[]{:S(2)}, u32[]{:S(2)}) collective-permute-start(bf16[256]{0:T(256)(128)(2,1)S(1)} %collective-permute-done.6), channel_id=1, source_target_pairs={{0,2},{1,3},{4,6},{5,7},{8,10},{9,11},{12,14},{13,15},{16,18},{17,... | collective-permute-start | bytes 1544 | tf_op jit(solution)/shard_map/ppermute | solution.py:14
  416.8 7.3 %collective-permute-start.1 = (bf16[256,128]{0,1:T(8,128)(2,1)S(1)}, bf16[256,128]{0,1:T(8,128)(2,1)S(1)}, u32[]{:S(2)}, u32[]{:S(2)}) collective-permute-start(bf16[256,128]{0,1:T(8,128)(2,1)S(1)} %collective-permute-done), channel_id=1, source_target_pairs={{2,0},{3,1},{6,4},{7,5},{10,8},{11,9},{14,12},{15,13},{18,16},{19,... | collective-permute-start | bytes 196616 | tf_op jit(solution)/shard_map/ppermute | solution.py:14
  422.2 7.7 %collective-permute-start.3 = (bf16[256,128]{0,1:T(8,128)(2,1)S(1)}, bf16[256,128]{0,1:T(8,128)(2,1)S(1)}, u32[]{:S(2)}, u32[]{:S(2)}) collective-permute-start(bf16[256,128]{0,1:T(8,128)(2,1)S(1)} %collective-permute-done.2), channel_id=1, source_target_pairs={{0,2},{1,3},{4,6},{5,7},{8,10},{9,11},{12,14},{13,15},{16,18},{17,... | collective-permute-start | bytes 196616 | tf_op jit(solution)/shard_map/ppermute | solution.py:14
Sparse Core Ops, SparseCore 0:
  14.9 113.4 all-gather.3
  129.9 91.1 all-gather.5
  222.6 37.4 all-gather.7
  286.0 111.1 reduce-scatter.1
where the time goes:
time: 438 us; the launch traced here: 437 us
  waiting for transfers between devices  323 us (74%)
  matrix products  50 us (11%)
  starting transfers between devices  22.2 us (5%)
  other arithmetic  17 us (4%)
  between operations  14.9 us (3%)
  local copies, waits for them, and re-layouts  9.9 us (2%)
    all_gather x1, waiting for transfers between devices, shards(): gathered = lax.all_gather(norm_in, 'seq', axis=0, tiled=True)  112 us
    reduce_scatter x1, waiting for transfers between devices, shards(): lax.psum_scatter(jnp.dot(attended, full_out, preferred_element_type=jnp.f...  111 us
    all_gather x1, waiting for transfers between devices, shards(): lax.all_gather(w_qkv, 'tile', axis=0, tiled=True)  92.7 us
    ppermute x8, starting transfers between devices, shifted(): lax.ppermute(value, axis, [(source, source + steps) for source in range(l...  22.1 us
    dot_general x1, matrix products, shards(): jnp.dot(gathered, lax.all_gather(w_qkv, 'tile', axis=0, tiled=True), pref...  19.6 us
    dot_general x2, matrix products, shards(): jnp.einsum('qhe,khe->hqk', queries[first:first + block], keys, preferred_...  10.9 us
    dot_general x1, matrix products, shards(): jnp.dot(attended, full_out, preferred_element_type=jnp.float32)  9.54 us
    dot_general x2, matrix products, shards(): jnp.einsum('hqk,khe->qhe', probs, values, preferred_element_type=jnp.floa...  8.92 us
  transfers between devices with their start and end apart: 12, of which 5 were waited for; matrix products, arithmetic and copies ran while one was open for 12% of the time, Pallas kernels for 0%

commit v1 on v0

--- a/solution.py
+++ b/solution.py
@@ -33,7 +33,12 @@
 def shards(hidden, modulation, w_qkv, w_out, w_head, latent, weights_int, step_index):
     local = hidden[0].astype(jnp.float32)
     norm_in = (layer_norm(local) * (1.0 + modulation[1]) + modulation[0]).astype(jnp.bfloat16)
-    gathered = lax.all_gather(norm_in, "seq", axis=0, tiled=True)
+    ring = [norm_in]
+    for hop in range(3):
+        ring.append(lax.ppermute(ring[-1], "seq", [(dev, (dev + 1) % 4) for dev in range(4)]))
+    gathered = jnp.roll(
+        jnp.concatenate(ring[::-1], axis=0), (lax.axis_index("seq") + 1) * ring[0].shape[0], axis=0
+    )
     length = gathered.shape[0]
     heads_here = w_qkv.shape[1] // (3 * HD)
     projected = jnp.dot(

time: 438 us -> 352 us (0.80)
  waiting for transfers between devices: 323 us -> 221 us
  local copies, waits for them, and re-layouts: 9.9 us -> 23.8 us
    all_gather x1 -> x0, waiting for transfers between devices: 112 us -> none  [shards(): gathered = lax.all_gather(norm_in, 'seq', axis=0, tiled=True)]
    ppermute x0 -> x3, waiting for transfers between devices: none -> 102 us  [shards(): lax.ppermute(ring[-1], 'seq', [(dev, (dev + 1) % 4) for dev in range(4)])]
    all_gather x1, waiting for transfers between devices: 92.7 us -> 0.01 us  [shards(): lax.all_gather(w_qkv, 'tile', axis=0, tiled=True)]
    unnamed x25 -> x43, local copies, waits for them, and re-layouts: 7.19 us -> 21 us
    ppermute x0 -> x3, starting transfers between devices: none -> 6.19 us  [shards(): lax.ppermute(ring[-1], 'seq', [(dev, (dev + 1) % 4) for dev in range(4)])]
  transfers between devices with their start and end apart: 12 -> 14, of which waited for: 5 -> 7; matrix products, arithmetic and copies ran while one was open for 12% -> 20% of each run, Pallas kernels for 0% -> 0%
where the time goes in v1:
time: 352 us; the launch traced here: 350 us
  waiting for transfers between devices  221 us (63%)
  matrix products  50.1 us (14%)
  starting transfers between devices  24.4 us (7%)
  local copies, waits for them, and re-layouts  23.8 us (7%)
  other arithmetic  15.7 us (4%)
  between operations  14.9 us (4%)
    reduce_scatter x1, waiting for transfers between devices, shards(): lax.psum_scatter(jnp.dot(attended, full_out, preferred_element_type=jnp.f...  112 us
    ppermute x3, waiting for transfers between devices, shards(): lax.ppermute(ring[-1], 'seq', [(dev, (dev + 1) % 4) for dev in range(4)])  102 us
    unnamed x43, local copies, waits for them, and re-layouts  21 us
    dot_general x1, matrix products, shards(): jnp.dot(gathered, lax.all_gather(w_qkv, 'tile', axis=0, tiled=True), pref...  19.6 us
    ppermute x8, starting transfers between devices, shifted(): lax.ppermute(value, axis, [(source, source + steps) for source in range(l...  18 us
    dot_general x2, matrix products, shards(): jnp.einsum('qhe,khe->hqk', queries[first:first + block], keys, preferred_...  10.9 us
    dot_general x1, matrix products, shards(): jnp.dot(attended, full_out, preferred_element_type=jnp.float32)  9.61 us
    dot_general x2, matrix products, shards(): jnp.einsum('hqk,khe->qhe', probs, values, preferred_element_type=jnp.floa...  8.92 us
  transfers between devices with their start and end apart: 14, of which 7 were waited for; matrix products, arithmetic and copies ran while one was open for 20% of the time, Pallas kernels for 0%

profile of v1, /device:TPU:26, one launch (start us, length us, event | category | flops | bytes accessed | tf_op | source)
XLA Modules:
  0.0 349.6 jit_solution(17918566632560923291)
XLA Ops:
  11.2 35.9 %collective-permute-done = bf16[256,3072]{1,0:T(8,128)(2,1)S(1)} collective-permute-done((bf16[256,3072]{1,0:T(8,128)(2,1)S(1)}, bf16[256,3072]{1,0:T(8,128)(2,1)S(1)}, u32[]{:S(2)}, u32[]{:S(2)}) %collective-permute-start) | collective-permute-done | bytes 1572896 | tf_op jit(solution)/shard_map/ppermute | solution.py:38
  47.2 2.1 collective-permute-start.1
  49.2 33.4 %collective-permute-done.1 = bf16[256,3072]{1,0:T(8,128)(2,1)} collective-permute-done((bf16[256,3072]{1,0:T(8,128)(2,1)S(1)}, bf16[256,3072]{1,0:T(8,128)(2,1)}, u32[]{:S(2)}, u32[]{:S(2)}) %collective-permute-start.1) | collective-permute-done | bytes 1572896 | tf_op jit(solution)/shard_map/ppermute | solution.py:38
  82.6 3.8 %collective-permute-start.2 = (bf16[256,3072]{1,0:T(8,128)(2,1)}, bf16[256,3072]{1,0:T(8,128)(2,1)}, u32[]{:S(2)}, u32[]{:S(2)}) collective-permute-start(bf16[256,3072]{1,0:T(8,128)(2,1)} %collective-permute-done.1), channel_id=1, source_target_pairs={{0,1},{1,2},{2,3},{3,0},{4,5},{5,6},{6,7},{7,4},{8,9},{9,10},{10,1... | collective-permute-start | bytes 4718600 | tf_op jit(solution)/shard_map/ppermute | solution.py:38
  86.6 32.2 %collective-permute-done.2 = bf16[256,3072]{1,0:T(8,128)(2,1)} collective-permute-done((bf16[256,3072]{1,0:T(8,128)(2,1)}, bf16[256,3072]{1,0:T(8,128)(2,1)}, u32[]{:S(2)}, u32[]{:S(2)}) %collective-permute-start.2) | collective-permute-done | bytes 1572896 | tf_op jit(solution)/shard_map/ppermute | solution.py:38
  118.8 2.7 constant_dynamic-update-slice_fusion.7
  121.5 2.7 constant_dynamic-update-slice_fusion.6
  125.4 1.9 constant_dynamic-update-slice_fusion.4
  127.3 2.7 constant_dynamic-update-slice_fusion.3
  130.0 2.7 constant_dynamic-update-slice_fusion.2
  132.7 1.3 constant_dynamic-update-slice_fusion.1
  134.0 2.0 constant_dynamic-update-slice_fusion
  136.0 19.6 %fusion.2 = f32[1024,2304]{0,1:T(8,128)S(1)} fusion(bf16[3072,2304]{1,0:T(8,128)(2,1)} %all-gather.3.cloned.1.call-done, bf16[2048,3072]{1,0:T(8,128)(2,1)} %constant_dynamic-update-slice_fusion, s32[]{:T(128)S(6)} %select_n.42), kind=kOutput, calls=%fused_computation.6 | convolution fusion | flops 14495514624 | bytes 29884420 | tf_op jit(solution)/shard_map/dot_general | solution.py:44
  155.6 3.5 %copy-done.3 = f32[1024,2304]{0,1:T(8,128)} copy-done((f32[1024,2304]{0,1:T(8,128)}, f32[1024,2304]{0,1:T(8,128)S(1)}, u32[]{:S(2)}) %copy-start.3) | copy-done | bytes 9437208
  159.2 2.1 slice.50
  161.3 3.5 %copy.21 = f32[1024,6,1,128]{3,0,1,2:T(8,128)} copy(f32[1024,6,1,128]{0,3,2,1:T(8,128)} %slice.50) | data formatting | bytes 6291456
  164.8 2.9 fusion.14
  167.8 2.3 multiply_reduce_fusion.1
  171.1 8.2 %fusion = (f32[6,512]{1,0:T(8,128)S(1)}, f32[6,512,1024]{2,1,0:T(8,128)}) fusion(f32[1024,6,3,128]{0,3,2,1:T(8,128)} %bitcast.81, f32[1024,6]{0,1:T(8,128)S(1)} %add_rsqrt_fusion, bf16[1024,6,128]{2,0,1:T(8,128)(2,1)S(1)} %fusion.15), kind=kOutput, calls=%fused_computation.4 | convolution fusion | flops 813167616 | bytes 16560128 | tf_op jit(solution)/shard_map/qhe,khe->hqk/dot_general | solution.py:59
  179.3 2.7 fusion.1
  182.0 6.0 %fusion.21 = bf16[512,6,128]{0,2,1:T(8,128)(2,1)S(1)} fusion(f32[6,512,1024]{2,1,0:T(8,128)} %get-tuple-element.14, f32[6,512]{1,0:T(8,128)S(1)} %get-tuple-element.13, f32[1024,6,3,128]{0,3,2,1:T(8,128)S(1)} %bitcast.85), kind=kOutput, calls=%fused_computation.37 | convolution fusion | flops 815136768 | bytes 14958592 | tf_op jit(solution)/shard_map/hqk,khe->qhe/dot_general | solution.py:70
  188.0 2.9 fusion.22
  191.2 9.6 %convolution_convert_fusion = bf16[1024,3072]{1,0:T(8,128)(2,1)} fusion(bf16[1024,768]{0,1:T(8,128)(2,1)S(1)} %bitcast.87, bf16[768,3072]{1,0:T(8,128)(2,1)} %all-gather.5.cloned.1.call-done), kind=kOutput, calls=%fused_computation.10 | convolution fusion | flops 4834983936 | bytes 12582912 | tf_op jit(solution)/shard_map/dot_general | solution.py:76
  201.6 111.6 %reduce-scatter.2.cloned.1.call-done = bf16[256,3072]{1,0:T(8,128)(2,1)} async-done(((bf16[1024,3072]{1,0:T(8,128)(2,1)}), bf16[256,3072]{1,0:T(8,128)(2,1)}) %reduce-scatter.2.cloned.1.call-update) | async-done | bytes 1572880 | tf_op jit(solution)/shard_map/reduce_scatter | solution.py:75
  313.2 2.1 fusion.16
  317.3 1.9 collective-permute-start.3
  319.3 3.6 %collective-permute-start.5 = (bf16[256,128]{0,1:T(8,128)(2,1)S(1)}, bf16[256,128]{0,1:T(8,128)(2,1)S(1)}, u32[]{:S(2)}, u32[]{:S(2)}) collective-permute-start(bf16[256,128]{0,1:T(8,128)(2,1)S(1)} %fusion.29), channel_id=1, source_target_pairs={{4,0},{8,4},{12,8},{5,1},{9,5},{13,9},{6,2},{10,6},{14,10},{7,3},{... | collective-permute-start | bytes 196616 | tf_op jit(solution)/shard_map/ppermute | solution.py:14
  322.9 1.9 collective-permute-start.9
  324.8 2.4 collective-permute-start.7
  329.7 4.3 %collective-permute-start.8 = (bf16[256]{0:T(256)(128)(2,1)S(1)}, bf16[256]{0:T(256)(128)(2,1)S(1)}, u32[]{:S(2)}, u32[]{:S(2)}) collective-permute-start(bf16[256]{0:T(256)(128)(2,1)S(1)} %collective-permute-done.7), channel_id=1, source_target_pairs={{2,0},{3,1},{6,4},{7,5},{10,8},{11,9},{14,12},{15,13},{18,16},{19,... | collective-permute-start | bytes 1544 | tf_op jit(solution)/shard_map/ppermute | solution.py:14
  334.0 1.3 collective-permute-start.4
  337.2 5.2 %collective-permute-done.6 = bf16[256,128]{0,1:T(8,128)(2,1)S(1)} collective-permute-done((bf16[256,128]{0,1:T(8,128)(2,1)S(1)}, bf16[256,128]{0,1:T(8,128)(2,1)S(1)}, u32[]{:S(2)}, u32[]{:S(2)}) %collective-permute-start.6) | collective-permute-done | bytes 65568 | tf_op jit(solution)/shard_map/ppermute | solution.py:14
  (75 shorter events, 13.6 us)
Async XLA Ops:
  7.2 309.0 %copy-start = (bf16[3072,64]{0,1:T(8,128)(2,1)S(1)}, bf16[3072,64]{0,1:T(8,128)(2,1)}, u32[]{:S(2)}) copy-start(bf16[3072,64]{0,1:T(8,128)(2,1)} %param.12) | copy-start | bytes 1179652
  7.2 1.5 copy-start.1
  7.2 2.3 copy-start.8
  7.2 128.8 %all-gather.3.cloned.1.call-start = ((), (), s32[]{:S(2)}) async-start(), calls=%async_computation.1 | async-start | bytes 17694720 | tf_op jit(solution)/shard_map/all_gather | solution.py:46
  7.9 183.2 %all-gather.5.cloned.1.call-start = ((), (), s32[]{:S(2)}) async-start(), calls=%async_computation.2 | async-start | bytes 5898240 | tf_op jit(solution)/shard_map/all_gather | solution.py:49
  9.5 0.7 copy-start.9
  10.2 72.5 %copy-start.5 = (f32[1,3072]{1,0:T(1,128)}, f32[1,3072]{1,0:T(1,128)S(1)}, u32[]{:S(2)}) copy-start(f32[1,3072]{1,0:T(1,128)S(1)} %get-tuple-element.8) | copy-start | bytes 36868
  11.0 36.2 %collective-permute-start = (bf16[256,3072]{1,0:T(8,128)(2,1)S(1)}, bf16[256,3072]{1,0:T(8,128)(2,1)S(1)}, u32[]{:S(2)}, u32[]{:S(2)}) collective-permute-start(bf16[256,3072]{1,0:T(8,128)(2,1)S(1)} %fusion.13), channel_id=1, source_target_pairs={{0,1},{1,2},{2,3},{3,0},{4,5},{5,6},{6,7},{7,4},{8,9},{9,10},{10,1... | collective-permute-start | bytes 4718600 | tf_op jit(solution)/shard_map/ppermute | solution.py:38
  47.2 35.5 %collective-permute-start.1 = (bf16[256,3072]{1,0:T(8,128)(2,1)S(1)}, bf16[256,3072]{1,0:T(8,128)(2,1)}, u32[]{:S(2)}, u32[]{:S(2)}) collective-permute-start(bf16[256,3072]{1,0:T(8,128)(2,1)S(1)} %collective-permute-done), channel_id=1, source_target_pairs={{0,1},{1,2},{2,3},{3,0},{4,5},{5,6},{6,7},{7,4},{8,9},{9,10},{10,1... | collective-permute-start | bytes 4718600 | tf_op jit(solution)/shard_map/ppermute | solution.py:38
  82.6 36.2 %collective-permute-start.2 = (bf16[256,3072]{1,0:T(8,128)(2,1)}, bf16[256,3072]{1,0:T(8,128)(2,1)}, u32[]{:S(2)}, u32[]{:S(2)}) collective-permute-start(bf16[256,3072]{1,0:T(8,128)(2,1)} %collective-permute-done.1), channel_id=1, source_target_pairs={{0,1},{1,2},{2,3},{3,0},{4,5},{5,6},{6,7},{7,4},{8,9},{9,10},{10,1... | collective-permute-start | bytes 4718600 | tf_op jit(solution)/shard_map/ppermute | solution.py:38
  86.5 226.7 %reduce-scatter.2.cloned.1.call-start = ((), (), s32[]{:S(2)}) async-start(), calls=%async_computation.3 | async-start | bytes 7864320 | tf_op jit(solution)/shard_map/reduce_scatter | solution.py:75
  121.5 3.9 %copy-start.6 = (f32[1,3072]{1,0:T(1,128)S(1)}, f32[1,3072]{1,0:T(1,128)}, u32[]{:S(2)}) copy-start(f32[1,3072]{1,0:T(1,128)} %copy-done.5) | copy-start | bytes 36868
  121.5 3.9 %copy-start.10 = (f32[256]{0:T(256)S(1)}, f32[256]{0:T(256)}, u32[]{:S(2)}) copy-start(f32[256]{0:T(256)} %copy-done.9) | copy-start | bytes 3076
  155.6 3.6 %copy-start.3 = (f32[1024,2304]{0,1:T(8,128)}, f32[1024,2304]{0,1:T(8,128)S(1)}, u32[]{:S(2)}) copy-start(f32[1024,2304]{0,1:T(8,128)S(1)} %fusion.2) | copy-start | bytes 28311556
  164.8 5.3 %copy-start.2 = (f32[1024,6,1,128]{3,0,1,2:T(8,128)S(1)}, f32[1024,6,1,128]{3,0,1,2:T(8,128)}, u32[]{:S(2)}) copy-start(f32[1024,6,1,128]{3,0,1,2:T(8,128)} %copy.21) | copy-start | bytes 9437188
  170.1 9.2 %slice-start = ((s8[9437184]{0:T(1024)(128)(4,1)}), s8[4194304]{0:T(1024)(128)(4,1)S(1)}, s32[]{:S(2)}) async-start(s8[9437184]{0:T(1024)(128)(4,1)} %bitcast.82), calls=%async_computation.4 | async-start | bytes 8388608
  171.1 8.2 %slice-start.1 = ((s8[9437184]{0:T(1024)(128)(4,1)}), s8[4194304]{0:T(1024)(128)(4,1)S(1)}, s32[]{:S(2)}) async-start(s8[9437184]{0:T(1024)(128)(4,1)} %bitcast.82), calls=%async_computation.5 | async-start | bytes 8388608
  171.1 8.2 %slice-start.2 = ((s8[9437184]{0:T(1024)(128)(4,1)}), s8[1048576]{0:T(1024)(128)(4,1)S(1)}, s32[]{:S(2)}) async-start(s8[9437184]{0:T(1024)(128)(4,1)} %bitcast.82), calls=%async_computation.6 | async-start | bytes 2097152
  200.8 0.7 copy-start.13
  200.8 112.4 %copy-start.7 = (f32[1,3072]{1,0:T(1,128)S(1)}, f32[1,3072]{1,0:T(1,128)}, u32[]{:S(2)}) copy-start(f32[1,3072]{1,0:T(1,128)} %get-tuple-element.6) | copy-start | bytes 36868
  313.2 2.2 copy-start.4
  313.2 3.0 copy-start.11
  313.2 3.0 copy-start.12
  313.2 3.0 copy-start.14
  317.3 16.7 %collective-permute-start.3 = (bf16[256,128]{0,1:T(8,128)(2,1)S(1)}, bf16[256,128]{0,1:T(8,128)(2,1)S(1)}, u32[]{:S(2)}, u32[]{:S(2)}) collective-permute-start(bf16[256,128]{0,1:T(8,128)(2,1)S(1)} %fusion.29), channel_id=1, source_target_pairs={{0,4},{4,8},{8,12},{1,5},{5,9},{9,13},{2,6},{6,10},{10,14},{3,7},{... | collective-permute-start | bytes 196616 | tf_op jit(solution)/shard_map/ppermute | solution.py:14
  319.3 16.1 %collective-permute-start.5 = (bf16[256,128]{0,1:T(8,128)(2,1)S(1)}, bf16[256,128]{0,1:T(8,128)(2,1)S(1)}, u32[]{:S(2)}, u32[]{:S(2)}) collective-permute-start(bf16[256,128]{0,1:T(8,128)(2,1)S(1)} %fusion.29), channel_id=1, source_target_pairs={{4,0},{8,4},{12,8},{5,1},{9,5},{13,9},{6,2},{10,6},{14,10},{7,3},{... | collective-permute-start | bytes 196616 | tf_op jit(solution)/shard_map/ppermute | solution.py:14
  322.9 4.3 %collective-permute-start.9 = (bf16[256]{0:T(256)(128)(2,1)S(1)}, bf16[256]{0:T(256)(128)(2,1)S(1)}, u32[]{:S(2)}, u32[]{:S(2)}) collective-permute-start(bf16[256]{0:T(256)(128)(2,1)S(1)} %convert_element_type.109), channel_id=1, source_target_pairs={{4,0},{8,4},{12,8},{5,1},{9,5},{13,9},{6,2},{10,6},{14,10},{7,3},{... | collective-permute-start | bytes 1544 | tf_op jit(solution)/shard_map/ppermute | solution.py:14
  324.8 4.9 %collective-permute-start.7 = (bf16[256]{0:T(256)(128)(2,1)S(1)}, bf16[256]{0:T(256)(128)(2,1)S(1)}, u32[]{:S(2)}, u32[]{:S(2)}) collective-permute-start(bf16[256]{0:T(256)(128)(2,1)S(1)} %convert_element_type.109), channel_id=1, source_target_pairs={{0,4},{4,8},{8,12},{1,5},{5,9},{9,13},{2,6},{6,10},{10,14},{3,7},{... | collective-permute-start | bytes 1544 | tf_op jit(solution)/shard_map/ppermute | solution.py:14
  327.3 9.4 %collective-permute-start.10 = (bf16[256]{0:T(256)(128)(2,1)S(1)}, bf16[256]{0:T(256)(128)(2,1)S(1)}, u32[]{:S(2)}, u32[]{:S(2)}) collective-permute-start(bf16[256]{0:T(256)(128)(2,1)S(1)} %collective-permute-done.9), channel_id=1, source_target_pairs={{0,2},{1,3},{4,6},{5,7},{8,10},{9,11},{12,14},{13,15},{16,18},{17,... | collective-permute-start | bytes 1544 | tf_op jit(solution)/shard_map/ppermute | solution.py:14
  329.7 6.9 %collective-permute-start.8 = (bf16[256]{0:T(256)(128)(2,1)S(1)}, bf16[256]{0:T(256)(128)(2,1)S(1)}, u32[]{:S(2)}, u32[]{:S(2)}) collective-permute-start(bf16[256]{0:T(256)(128)(2,1)S(1)} %collective-permute-done.7), channel_id=1, source_target_pairs={{2,0},{3,1},{6,4},{7,5},{10,8},{11,9},{14,12},{15,13},{18,16},{19,... | collective-permute-start | bytes 1544 | tf_op jit(solution)/shard_map/ppermute | solution.py:14
  334.0 3.2 collective-permute-start.4
  335.4 7.1 %collective-permute-start.6 = (bf16[256,128]{0,1:T(8,128)(2,1)S(1)}, bf16[256,128]{0,1:T(8,128)(2,1)S(1)}, u32[]{:S(2)}, u32[]{:S(2)}) collective-permute-start(bf16[256,128]{0,1:T(8,128)(2,1)S(1)} %collective-permute-done.5), channel_id=1, source_target_pairs={{0,2},{1,3},{4,6},{5,7},{8,10},{9,11},{12,14},{13,15},{16,18},{17,... | collective-permute-start | bytes 196616 | tf_op jit(solution)/shard_map/ppermute | solution.py:14
Sparse Core Ops, SparseCore 0:
  9.6 91.0 all-gather.2
  102.2 37.4 all-gather.4
  200.9 112.2 reduce-scatter.1
